TPU v7x, 256 devices: a whole 4x4x8 slice. The times are simulated.
256 devices in a mesh: grp: 2 (over core), tok: 32 (over z, y), head: 4 (over x).
Axes of the slice: x: 4, y: 4, z: 8, core: 2. Of those that a mesh axis runs over, the one named last changes fastest.
Arguments:
- hidden_in: bfloat16 [2, 4096, 2560], P('grp', 'tok', 'head'), may hold values from -6 to 6
- attn_gain: bfloat16 [2560], replicated, may hold values from 0.5 to 1.5
- w_query: bfloat16 [2560, 2560], P('grp', 'head'), may hold values from -0.125 to 0.125
- key_projection_weight: bfloat16 [2560, 512], P('grp', 'head'), may hold values from -0.25 to 0.25
- value_projection_weight: bfloat16 [2560, 512], P('grp', 'head'), may hold values from -0.125 to 0.125
- w_out: bfloat16 [2560, 2560], P('grp', 'head'), may hold values from -0.125 to 0.125
- prefix_keys: bfloat16 [2, 2048, 4, 128], P('grp', 'tok', 'head'), may hold values from -91 to 91
- cached_prefix_values: bfloat16 [2, 2048, 4, 128], P('grp', 'tok', 'head'), may hold values from -6 to 6
- request_lengths: int32 [2, 16], P('grp'), may hold values from 1 to 1024, 4096 in all within a row
- moe_gain: bfloat16 [2560], replicated, may hold values from 0.5 to 1.5
- expert_ids: int32 [2, 4096, 6], P('grp', 'tok'), may hold values from 0 to 63, all different within a row; in each aligned block of 128 rows (0 to 127, 128 to 255, ..., all dimensions but the last counted through in order) at most 16 rows name the same one
- route_weights: float32 [2, 4096, 6], P('grp', 'tok'), may hold values from 0.05 to 0.3
- w_gate: bfloat16 [64, 2560, 1536], P(('grp', 'tok'), None, 'head'), may hold values from -0.125 to 0.125
- w_up: bfloat16 [64, 2560, 1536], P(('grp', 'tok'), None, 'head'), may hold values from -0.125 to 0.125
- w_down: bfloat16 [64, 1536, 2560], P(('grp', 'tok'), None, 'head'), may hold values from -0.15625 to 0.15625
Outputs:
- hidden_out: bfloat16 [2, 4096, 2560], P('grp', 'tok', 'head')
Inputs may be any that keep to these rules, and one draw needn't show every extreme that they name: `expert_ids`: each token names 6 different experts. Among the tokens of one device (aligned blocks of 128 tokens of a group) no expert is named more than 16 times.
All inputs are finite; a program needn't handle non-finite values.
Results may differ from a plain program's by a relative error of at most 0.011.
Values may be sent and summed in bfloat16 or wider, within the bound.
A program may use at most 64 MiB of HBM per device.

v0:
```python
import math
import jax
import jax.numpy as jnp
from jax import lax
from jax.sharding import PartitionSpec as P

ROPE_BASE = 500000.0
NORM_EPS = 1e-06
MASKED = -1e30


def shifted(block, axis, distance):
    devices = range(lax.axis_size(axis))
    route = [(i - distance, i) for i in devices if i - distance in devices]
    return lax.ppermute(block, axis, route)


def rms_norm(values_in, gain_vector):
    widened = values_in.astype(jnp.float32)
    mean_sq = jnp.mean(widened * widened, axis=-1, keepdims=True)
    return (widened * lax.rsqrt(mean_sq + NORM_EPS) * gain_vector.astype(jnp.float32)).astype(
        jnp.bfloat16
    )


def apply_rotary(product, token_positions):
    half_dim = product.shape[-1] // 2
    frequency = jnp.exp(
        jnp.arange(half_dim, dtype=jnp.float32) * (-2.0 * math.log(ROPE_BASE) / product.shape[-1])
    )
    angles = token_positions.astype(jnp.float32)[:, None] * frequency[None, :]
    cosine = jnp.cos(angles)[:, None, :]
    sine_part = jnp.sin(angles)[:, None, :]
    first_half = product[..., :half_dim]
    second_half = product[..., half_dim:]
    turned = jnp.concatenate(
        [
            first_half * cosine - second_half * sine_part,
            second_half * cosine + first_half * sine_part,
        ],
        axis=-1,
    )
    return turned.astype(jnp.bfloat16)


def attend(running, queries, keys_block, values_block, visible):
    row_max, row_total, summed = running
    scores = jnp.einsum(
        "tcrd,kcd->ctrk", queries, keys_block, preferred_element_type=jnp.float32
    ) * queries.shape[-1] ** (-0.5)
    if visible is not None:
        scores = jnp.where(visible[None, :, None, :], scores, MASKED)
    new_max = jnp.maximum(row_max, jnp.max(scores, axis=-1))
    weights = jnp.exp(scores - new_max[..., None])
    if visible is not None:
        weights = jnp.where(visible[None, :, None, :], weights, 0.0)
    factor = jnp.exp(row_max - new_max)
    row_total = row_total * factor + jnp.sum(weights, axis=-1)
    summed = summed * factor[..., None] + jnp.einsum(
        "ctrk,kcd->ctrd",
        weights.astype(jnp.bfloat16),
        values_block,
        preferred_element_type=jnp.float32,
    )
    return (new_max, row_total, summed)


def on_device(
    hidden_in,
    attn_gain,
    w_query,
    key_projection_weight,
    value_projection_weight,
    w_out,
    prefix_keys,
    cached_prefix_values,
    request_lengths,
    moe_gain,
    expert_ids,
    route_weights,
    w_gate,
    w_up,
    w_down,
):
    tok_count = lax.axis_size("tok")
    grp_count = lax.axis_size("grp")
    tok_rank = lax.axis_index("tok")
    head_rank = lax.axis_index("head")
    tok_dev = hidden_in.shape[1]
    model_width = attn_gain.shape[0]
    head_dim = prefix_keys.shape[3]
    kv_local = prefix_keys.shape[2]
    group_length = w_query.shape[1] // (kv_local * head_dim)
    prefix_total = prefix_keys.shape[1] * tok_count
    quarter = hidden_in[0]
    features = lax.all_gather(quarter, "head", axis=1, tiled=True)
    attention_input = rms_norm(features, attn_gain)
    lengths = request_lengths[0]
    request_ends = jnp.cumsum(lengths)
    starts = request_ends - lengths
    token_index = tok_rank * tok_dev + jnp.arange(tok_dev, dtype=jnp.int32)
    own_start = jnp.max(
        jnp.where(starts[None, :] <= token_index[:, None], starts[None, :], 0), axis=1
    )
    token_positions = prefix_total + token_index - own_start
    full_query, full_key, full_value, full_out = (
        lax.all_gather(w_query, "grp", axis=0, tiled=True),
        lax.all_gather(key_projection_weight, "grp", axis=0, tiled=True),
        lax.all_gather(value_projection_weight, "grp", axis=0, tiled=True),
        lax.all_gather(w_out, "grp", axis=0, tiled=True),
    )
    query_product = jnp.dot(attention_input, full_query, preferred_element_type=jnp.float32)
    key_product = jnp.dot(attention_input, full_key, preferred_element_type=jnp.float32)
    value_product = jnp.dot(attention_input, full_value, preferred_element_type=jnp.float32)
    queries = apply_rotary(
        query_product.reshape(tok_dev, kv_local * group_length, head_dim), token_positions
    )
    queries = queries.reshape(tok_dev, kv_local, group_length, head_dim)
    request_suffix_keys = apply_rotary(
        key_product.reshape(tok_dev, kv_local, head_dim), token_positions
    )
    request_suffix_values = value_product.astype(jnp.bfloat16).reshape(tok_dev, kv_local, head_dim)
    running = (
        jnp.full((kv_local, tok_dev, group_length), MASKED, jnp.float32),
        jnp.zeros((kv_local, tok_dev, group_length), jnp.float32),
        jnp.zeros((kv_local, tok_dev, group_length, head_dim), jnp.float32),
    )
    running = attend(
        running,
        queries,
        lax.all_gather(prefix_keys[0], "tok", axis=0, tiled=True),
        lax.all_gather(cached_prefix_values[0], "tok", axis=0, tiled=True),
        None,
    )

    def visible_from(first_index, count):
        key_index = first_index + jnp.arange(count, dtype=jnp.int32)
        return (key_index[None, :] >= own_start[:, None]) & (
            key_index[None, :] <= token_index[:, None]
        )

    running = attend(
        running,
        queries,
        request_suffix_keys,
        request_suffix_values,
        visible_from(tok_rank * tok_dev, tok_dev),
    )
    longest = tok_dev * tok_count // 4
    reach_devices = (longest - 1 + tok_dev - 1) // tok_dev
    stacked = jnp.stack([request_suffix_keys, request_suffix_values])
    for distance in range(1, reach_devices + 1):
        arrived = shifted(stacked, "tok", distance)
        running = attend(
            running,
            queries,
            arrived[0],
            arrived[1],
            visible_from((tok_rank - distance) * tok_dev, tok_dev),
        )
    row_max, row_total, summed = running
    attended = (summed / row_total[..., None]).astype(jnp.bfloat16)
    attended = jnp.transpose(attended, (1, 0, 2, 3)).reshape(
        tok_dev, kv_local * group_length * head_dim
    )
    partial_value = lax.dot_general(
        attended, full_out, (((1,), (1,)), ((), ())), preferred_element_type=jnp.float32
    )
    share_width = model_width // lax.axis_size("head")
    mixed_sum = lax.psum(partial_value.astype(jnp.bfloat16), "head").astype(jnp.float32)
    mid_full = (features.astype(jnp.float32) + mixed_sum).astype(jnp.bfloat16)
    mid_quarter = lax.dynamic_slice_in_dim(mid_full, head_rank * share_width, share_width, 1)
    moe_in = rms_norm(mid_full, moe_gain)
    experts = grp_count * tok_count * w_gate.shape[0]
    top_count = expert_ids.shape[2]
    capacity = 4 * tok_dev * top_count // (3 * experts)
    chosen = expert_ids[0].reshape(-1)
    onehot = (chosen[:, None] == jnp.arange(experts, dtype=jnp.int32)[None, :]).astype(jnp.int32)
    slot_rank = jnp.sum(onehot * jnp.cumsum(onehot, axis=0), axis=1) - 1
    slot_place = chosen * capacity + slot_rank
    choice_token = jnp.arange(tok_dev * top_count, dtype=jnp.int32) // top_count
    source = jnp.full((experts * capacity,), tok_dev, jnp.int32).at[slot_place].set(choice_token)
    outgoing = jnp.take(moe_in, source, axis=0, mode="fill", fill_value=0).reshape(
        experts, capacity, model_width
    )
    incoming = lax.all_to_all(outgoing, ("grp", "tok"), split_axis=0, concat_axis=0, tiled=True)
    flat_rows = incoming.reshape(-1, model_width)
    gate_act = jnp.dot(flat_rows, w_gate[0], preferred_element_type=jnp.float32)
    up_act = jnp.dot(flat_rows, w_up[0], preferred_element_type=jnp.float32)
    hidden = (jax.nn.silu(gate_act) * up_act).astype(jnp.bfloat16)
    down_rows = w_down[0]
    result = jnp.dot(
        lax.all_gather(hidden, "head", axis=1, tiled=True),
        down_rows,
        preferred_element_type=jnp.float32,
    )
    expert_out = result.astype(jnp.bfloat16).reshape(
        incoming.shape[0], incoming.shape[1], w_down.shape[2]
    )
    returned = lax.all_to_all(expert_out, ("grp", "tok"), split_axis=0, concat_axis=0, tiled=True)
    returned = returned.reshape(experts * capacity, share_width)
    picked = jnp.take(returned, slot_place, axis=0).astype(jnp.float32)
    weighted = jnp.sum(
        (picked * route_weights[0].reshape(-1)[:, None]).reshape(tok_dev, top_count, share_width),
        axis=1,
    )
    output = (mid_quarter.astype(jnp.float32) + weighted).astype(jnp.bfloat16)
    return output[None]


def solution(mesh):
    return jax.shard_map(
        on_device,
        mesh=mesh,
        in_specs=(
            P("grp", "tok", "head"),
            P(),
            P("grp", "head"),
            P("grp", "head"),
            P("grp", "head"),
            P("grp", "head"),
            P("grp", "tok", "head", None),
            P("grp", "tok", "head", None),
            P("grp", None),
            P(),
            P("grp", "tok", None),
            P("grp", "tok", None),
            P(("grp", "tok"), None, "head"),
            P(("grp", "tok"), None, "head"),
            P(("grp", "tok"), None, "head"),
        ),
        out_specs=P("grp", "tok", "head"),
        check_vma=False,
    )
```

profile of v0, /device:TPU:1, one launch (start us, length us, event | category | flops | bytes accessed | tf_op | source)
XLA Modules:
  0.0 505.7 jit_solution(13813160702682913209)
XLA Ops:
  9.6 13.2 %all-gather = bf16[1,128,2560]{2,1,0:T(8,128)(2,1)S(1)} all-gather(bf16[1,128,640]{2,1,0:T(8,128)(2,1)} %param.15), channel_id=2, replica_groups=mesh['grp'=2,'tok'=32,'head'=4] {'head'}, dimensions={2}, use_global_device_ids=true | all-gather | bytes 819200 | tf_op jit(solution)/shard_map/all_gather | solution.py:96
  23.1 6.3 %all_gather.28 = bf16[2560,128]{1,0:T(8,128)(2,1)S(1)} all-gather(bf16[1280,128]{1,0:T(8,128)(2,1)S(1)} %copy-done.2), channel_id=1, replica_groups=mesh['grp'=2,'tok'=32,'head'=4] {'grp'}, dimensions={0}, use_global_device_ids=true | all-gather | bytes 983040 | tf_op jit(solution)/shard_map/all_gather | solution.py:108
  29.4 2.3 all_gather.29
  33.6 1.9 collective-permute-start
  35.5 4.6 collective-permute-start.1
  40.1 4.3 collective-permute-start.2
  44.4 3.6 collective-permute-start.3
  48.0 3.9 collective-permute-start.4
  57.8 39.5 %all-gather.1 = bf16[1,2048,1,128]{3,1,2,0:T(8,128)(2,1)S(1)} all-gather(bf16[1,64,1,128]{3,1,2,0:T(8,128)(2,1)S(1)} %copy-done.19), channel_id=3, replica_groups=mesh['grp'=2,'tok'=32,'head'=4] {'tok'}, dimensions={1}, use_global_device_ids=true | all-gather | bytes 540672 | tf_op jit(solution)/shard_map/all_gather | solution.py:131
  97.3 39.7 %all-gather.2 = bf16[1,2048,1,128]{3,1,2,0:T(8,128)(2,1)} all-gather(bf16[1,64,1,128]{3,1,2,0:T(8,128)(2,1)S(1)} %copy-done.20), channel_id=4, replica_groups=mesh['grp'=2,'tok'=32,'head'=4] {'tok'}, dimensions={1}, use_global_device_ids=true | all-gather | bytes 540672 | tf_op jit(solution)/shard_map/all_gather | solution.py:132
  137.6 1.8 reduce-window.9
  141.3 1.6 compare_and_fusion.8
  142.9 3.4 fusion.156
  147.0 1.1 copy.185
  148.1 1.8 copy.186
  149.9 1.1 subtract_convert_fusion
  152.1 3.0 collective-permute-start.5
  155.2 1.0 fusion.169
  156.2 4.6 collective-permute-start.6
  160.8 1.0 fusion.168
  161.9 3.4 collective-permute-start.7
  165.2 1.0 fusion.167
  166.3 1.0 fusion.166
  167.3 1.0 fusion.165
  170.1 1.0 fusion
  172.1 1.0 fusion.90
  173.2 1.0 fusion.88
  174.1 1.0 fusion.86
  175.8 1.2 fusion.52
  177.2 1.1 fusion.55
  178.4 4.0 convolution_convert_fusion
  182.5 3.4 scatter_custom_fusion
  186.0 66.5 %all-reduce.2.cloned.1.call-done = bf16[128,2560]{1,0:T(8,128)(2,1)} async-done(((bf16[128,2560]{1,0:T(8,128)(2,1)}), bf16[128,2560]{1,0:T(8,128)(2,1)}) %all-reduce.2.cloned.1.call-update) | async-done | bytes 655376 | tf_op jit(solution)/shard_map/psum | solution.py:170
  252.6 2.2 fusion.17
  254.8 1.3 fusion.19
  256.1 6.3 %gather_fusion = bf16[1024,2560]{1,0:T(8,128)(2,1)} fusion(bf16[128,2560]{1,0:T(8,128)(2,1)S(1)} %fusion.19, s32[1024]{0:T(1024)S(1)} %fusion.138), kind=kCustom, calls=%fused_computation | custom fusion | bytes 10489856 | tf_op jit(solution)/shard_map/jit(_take)/gather | solution.py:183
  262.4 2.9 broadcast_select_fusion
  265.3 130.5 %all_to_all.10 = bf16[64,16,2560]{2,1,0:T(8,128)(2,1)S(1)} all-to-all(bf16[64,16,2560]{2,1,0:T(8,128)(2,1)S(1)} %broadcast_select_fusion), channel_id=1, replica_groups=mesh['grp'=2,'tok'=32,'head'=4] {'grp','tok'}, dimensions={0} | all-to-all | bytes 10485760 | tf_op jit(solution)/shard_map/all_to_all | solution.py:186
  395.8 2.9 fusion.10
  398.7 3.8 multiply_convert_fusion
  402.6 38.6 %all-gather.11.cloned.1.call-done = bf16[1024,1536]{1,0:T(8,128)(2,1)} async-done(((bf16[1024,384]{1,0:T(8,128)(2,1)}), bf16[1024,1536]{1,0:T(8,128)(2,1)}) %all-gather.11.cloned.1.call-update) | async-done | bytes 3145744 | tf_op jit(solution)/shard_map/all_gather | solution.py:193
  441.2 5.6 %fusion.12 = bf16[1024,640]{1,0:T(8,128)(2,1)} fusion(bf16[1024,1536]{1,0:T(8,128)(2,1)} %all-gather.11.cloned.1.call-done, bf16[1,1536,640]{2,1,0:T(8,128)(2,1)S(1)} %copy-done), kind=kOutput, calls=%fused_computation.24 | convolution fusion | flops 2013921280 | bytes 6422528 | tf_op jit(solution)/shard_map/dot_general | solution.py:192
  446.7 10.9 %all-to-all-start.1 = ((bf16[64,16,640]{2,1,0:T(8,128)(2,1)}), bf16[64,16,640]{2,1,0:T(8,128)(2,1)S(1)}, u32[]{:S(2)}, u32[]{:S(2)}) async-start(bf16[64,16,640]{2,1,0:T(8,128)(2,1)} %bitcast.201), calls=%async_computation.1 | async-start | bytes 2621440 | tf_op jit(solution)/shard_map/all_to_all | solution.py:200
  458.2 32.9 %all-to-all-done.1 = bf16[64,16,640]{2,1,0:T(8,128)(2,1)S(1)} async-done(((bf16[64,16,640]{2,1,0:T(8,128)(2,1)}), bf16[64,16,640]{2,1,0:T(8,128)(2,1)S(1)}, u32[]{:S(2)}, u32[]{:S(2)}) %all-to-all-start.1) | async-done | bytes 1310752 | tf_op jit(solution)/shard_map/all_to_all | solution.py:200
  491.0 3.4 gather_fusion.1
  494.4 2.1 gather.15
  496.5 1.0 multiply_reduce_fusion.1
  497.5 1.6 fusion.96
  (141 shorter events, 19.6 us)
Async XLA Ops:
  6.5 434.6 %copy-start = (bf16[1,1536,640]{2,1,0:T(8,128)(2,1)S(1)}, bf16[1,1536,640]{2,1,0:T(8,128)(2,1)}, u32[]{:S(2)}) copy-start(bf16[1,1536,640]{2,1,0:T(8,128)(2,1)} %param.29) | copy-start | bytes 5898244
  6.5 16.6 %copy-start.2 = (bf16[1280,128]{1,0:T(8,128)(2,1)S(1)}, bf16[1280,128]{1,0:T(8,128)(2,1)}, u32[]{:S(2)}) copy-start(bf16[1280,128]{1,0:T(8,128)(2,1)} %param.18) | copy-start | bytes 983044
  6.5 22.8 %copy-start.3 = (bf16[1280,128]{1,0:T(8,128)(2,1)S(1)}, bf16[1280,128]{1,0:T(8,128)(2,1)}, u32[]{:S(2)}) copy-start(bf16[1280,128]{1,0:T(8,128)(2,1)} %param.19) | copy-start | bytes 983044
  6.5 136.4 %all-gather.7.cloned.1.call-start = ((), (), s32[]{:S(2)}) async-start(), calls=%async_computation.2 | async-start | bytes 4915200 | tf_op jit(solution)/shard_map/all_gather | solution.py:107
  7.3 171.2 %all-gather.9.cloned.1.call-start = ((), (), s32[]{:S(2)}) async-start(), calls=%async_computation.3 | async-start | bytes 4915200 | tf_op jit(solution)/shard_map/all_gather | solution.py:110
  8.0 24.4 %copy-start.15 = (f32[2560]{0:T(1024)}, f32[2560]{0:T(1024)S(1)}, u32[]{:S(2)}) copy-start(f32[2560]{0:T(1024)S(1)} %convert_element_type.128) | copy-start | bytes 30724
  8.9 0.7 copy-start.24
  9.6 22.5 %copy-start.25 = (s32[128]{0:T(128)}, s32[128]{0:T(128)S(1)}, u32[]{:S(2)}) copy-start(s32[128]{0:T(128)S(1)} %select_reduce_fusion) | copy-start | bytes 1540
  31.7 20.3 %copy-start.26 = (f32[128]{0:T(128)}, f32[128]{0:T(128)S(1)}, u32[]{:S(2)}) copy-start(f32[128]{0:T(128)S(1)} %add_rsqrt_fusion.1) | copy-start | bytes 1540
  32.2 20.8 %copy-start.17 = (s32[1,128,6]{1,0,2:T(1,128)S(1)}, s32[1,128,6]{1,0,2:T(1,128)}, u32[]{:S(2)}) copy-start(s32[1,128,6]{1,0,2:T(1,128)} %param.25) | copy-start | bytes 9220
  32.2 25.6 %copy-start.19 = (bf16[1,64,1,128]{3,1,2,0:T(8,128)(2,1)S(1)}, bf16[1,64,1,128]{3,1,2,0:T(8,128)(2,1)}, u32[]{:S(2)}) copy-start(bf16[1,64,1,128]{3,1,2,0:T(8,128)(2,1)} %param.21) | copy-start | bytes 49156
  32.4 0.6 copy-start.8
  32.4 1.2 copy-start.10
  32.4 64.8 %copy-start.20 = (bf16[1,64,1,128]{3,1,2,0:T(8,128)(2,1)S(1)}, bf16[1,64,1,128]{3,1,2,0:T(8,128)(2,1)}, u32[]{:S(2)}) copy-start(bf16[1,64,1,128]{3,1,2,0:T(8,128)(2,1)} %param.22) | copy-start | bytes 49156
  32.9 2.6 copy-start.12
  32.9 104.1 %copy-start.22 = (bf16[2560]{0:T(1024)(128)(2,1)S(1)}, bf16[2560]{0:T(1024)(128)(2,1)}, u32[]{:S(2)}) copy-start(bf16[2560]{0:T(1024)(128)(2,1)} %param.24) | copy-start | bytes 15364
  33.6 118.5 %collective-permute-start = (bf16[2,128,1,128]{1,3,2,0:T(8,128)(2,1)}, bf16[2,128,1,128]{1,3,2,0:T(8,128)(2,1)}, u32[]{:S(2)}, u32[]{:S(2)}) collective-permute-start(bf16[2,128,1,128]{1,3,2,0:T(8,128)(2,1)} %pad_maximum_fusion.1), channel_id=1, source_target_pairs={{0,4},{4,8},{8,12},{12,16},{16,20},{20,24},{24,28},{28,32},{32,36}... | collective-permute-start | bytes 196616 | tf_op jit(solution)/shard_map/ppermute | solution.py:15
  35.5 120.7 %collective-permute-start.1 = (bf16[2,128,1,128]{1,3,2,0:T(8,128)(2,1)}, bf16[2,128,1,128]{1,3,2,0:T(8,128)(2,1)}, u32[]{:S(2)}, u32[]{:S(2)}) collective-permute-start(bf16[2,128,1,128]{1,3,2,0:T(8,128)(2,1)} %pad_maximum_fusion.1), channel_id=1, source_target_pairs={{0,8},{4,12},{8,16},{12,20},{16,24},{20,28},{24,32},{28,36},{32,40... | collective-permute-start | bytes 196616 | tf_op jit(solution)/shard_map/ppermute | solution.py:15
  40.1 121.7 %collective-permute-start.2 = (bf16[2,128,1,128]{1,3,2,0:T(8,128)(2,1)}, bf16[2,128,1,128]{1,3,2,0:T(8,128)(2,1)}, u32[]{:S(2)}, u32[]{:S(2)}) collective-permute-start(bf16[2,128,1,128]{1,3,2,0:T(8,128)(2,1)} %pad_maximum_fusion.1), channel_id=1, source_target_pairs={{0,12},{4,16},{8,20},{12,24},{16,28},{20,32},{24,36},{28,40},{32,4... | collective-permute-start | bytes 196616 | tf_op jit(solution)/shard_map/ppermute | solution.py:15
  44.4 121.8 %collective-permute-start.3 = (bf16[2,128,1,128]{1,3,2,0:T(8,128)(2,1)}, bf16[2,128,1,128]{1,3,2,0:T(8,128)(2,1)}, u32[]{:S(2)}, u32[]{:S(2)}) collective-permute-start(bf16[2,128,1,128]{1,3,2,0:T(8,128)(2,1)} %pad_maximum_fusion.1), channel_id=1, source_target_pairs={{0,16},{4,20},{8,24},{12,28},{16,32},{20,36},{24,40},{28,44},{32,4... | collective-permute-start | bytes 196616 | tf_op jit(solution)/shard_map/ppermute | solution.py:15
  48.0 119.3 %collective-permute-start.4 = (bf16[2,128,1,128]{1,3,2,0:T(8,128)(2,1)}, bf16[2,128,1,128]{1,3,2,0:T(8,128)(2,1)}, u32[]{:S(2)}, u32[]{:S(2)}) collective-permute-start(bf16[2,128,1,128]{1,3,2,0:T(8,128)(2,1)} %pad_maximum_fusion.1), channel_id=1, source_target_pairs={{0,20},{4,24},{8,28},{12,32},{16,36},{20,40},{24,44},{28,48},{32,5... | collective-permute-start | bytes 196616 | tf_op jit(solution)/shard_map/ppermute | solution.py:15
  52.0 200.6 %all-reduce.2.cloned.1.call-start = ((), (), s32[]{:S(2)}) async-start(), calls=%async_computation.4 | async-start | bytes 1310720 | tf_op jit(solution)/shard_map/psum | solution.py:170
  151.1 9.7 %copy-start.7 = (pred[128,128]{0,1:T(8,128)(4,1)S(1)}, pred[128,128]{0,1:T(8,128)(4,1)}, u32[]{:S(2)}) copy-start(pred[128,128]{0,1:T(8,128)(4,1)} %get-tuple-element.42) | copy-start | bytes 49156
  151.2 14.1 %copy-start.6 = (pred[128,128]{0,1:T(8,128)(4,1)S(1)}, pred[128,128]{0,1:T(8,128)(4,1)}, u32[]{:S(2)}) copy-start(pred[128,128]{0,1:T(8,128)(4,1)} %get-tuple-element.35) | copy-start | bytes 49156
  151.2 15.1 %copy-start.5 = (pred[128,128]{0,1:T(8,128)(4,1)S(1)}, pred[128,128]{0,1:T(8,128)(4,1)}, u32[]{:S(2)}) copy-start(pred[128,128]{0,1:T(8,128)(4,1)} %get-tuple-element.36) | copy-start | bytes 49156
  152.1 15.2 %copy-start.4 = (pred[128,128]{0,1:T(8,128)(4,1)S(1)}, pred[128,128]{0,1:T(8,128)(4,1)}, u32[]{:S(2)}) copy-start(pred[128,128]{0,1:T(8,128)(4,1)} %get-tuple-element.37) | copy-start | bytes 49156
  152.1 16.8 %copy-start.9 = (bf16[128,1,64]{0,2,1:T(8,128)(2,1)S(1)}, bf16[128,1,64]{0,2,1:T(8,128)(2,1)}, u32[]{:S(2)}) copy-start(bf16[128,1,64]{0,2,1:T(8,128)(2,1)} %copy-done.8) | copy-start | bytes 49156
  152.1 16.8 %copy-start.11 = (bf16[128,1,64]{0,2,1:T(8,128)(2,1)S(1)}, bf16[128,1,64]{0,2,1:T(8,128)(2,1)}, u32[]{:S(2)}) copy-start(bf16[128,1,64]{0,2,1:T(8,128)(2,1)} %copy-done.10) | copy-start | bytes 49156
  152.1 16.2 %collective-permute-start.5 = (bf16[2,128,1,128]{1,3,2,0:T(8,128)(2,1)}, bf16[2,128,1,128]{1,3,2,0:T(8,128)(2,1)S(1)}, u32[]{:S(2)}, u32[]{:S(2)}) collective-permute-start(bf16[2,128,1,128]{1,3,2,0:T(8,128)(2,1)} %pad_maximum_fusion.1), channel_id=1, source_target_pairs={{0,24},{4,28},{8,32},{12,36},{16,40},{20,44},{24,48},{28,52},{32,5... | collective-permute-start | bytes 196616 | tf_op jit(solution)/shard_map/ppermute | solution.py:15
  156.2 12.4 %collective-permute-start.6 = (bf16[2,128,1,128]{1,3,2,0:T(8,128)(2,1)}, bf16[2,128,1,128]{1,3,2,0:T(8,128)(2,1)S(1)}, u32[]{:S(2)}, u32[]{:S(2)}) collective-permute-start(bf16[2,128,1,128]{1,3,2,0:T(8,128)(2,1)} %pad_maximum_fusion.1), channel_id=1, source_target_pairs={{0,28},{4,32},{8,36},{12,40},{16,44},{20,48},{24,52},{28,56},{32,6... | collective-permute-start | bytes 196616 | tf_op jit(solution)/shard_map/ppermute | solution.py:15
  161.9 7.3 %collective-permute-start.7 = (bf16[2,128,1,128]{1,3,2,0:T(8,128)(2,1)}, bf16[2,128,1,128]{1,3,2,0:T(8,128)(2,1)S(1)}, u32[]{:S(2)}, u32[]{:S(2)}) collective-permute-start(bf16[2,128,1,128]{1,3,2,0:T(8,128)(2,1)} %pad_maximum_fusion.1), channel_id=1, source_target_pairs={{0,32},{4,36},{8,40},{12,44},{16,48},{20,52},{24,56},{28,60},{32,6... | collective-permute-start | bytes 196616 | tf_op jit(solution)/shard_map/ppermute | solution.py:15
  172.1 3.7 copy-start.1
  175.8 1.2 copy-start.13
  178.4 4.1 copy-start.16
  178.4 4.1 copy-start.21
  182.4 72.4 %copy-start.14 = (f32[2560]{0:T(1024)S(1)}, f32[2560]{0:T(1024)}, u32[]{:S(2)}) copy-start(f32[2560]{0:T(1024)} %convert_element_type.149) | copy-start | bytes 30724
  182.4 258.7 %all-gather.11.cloned.1.call-start = ((), (), s32[]{:S(2)}) async-start(), calls=%async_computation.5 | async-start | bytes 3932160 | tf_op jit(solution)/shard_map/all_gather | solution.py:193
  265.3 130.5 %copy-start.27 = (bf16[1,2560,384]{2,1,0:T(8,128)(2,1)S(1)}, bf16[1,2560,384]{2,1,0:T(8,128)(2,1)}, u32[]{:S(2)}) copy-start(bf16[1,2560,384]{2,1,0:T(8,128)(2,1)} %param.27) | copy-start | bytes 5898244
  395.8 2.9 copy-start.28
  446.7 11.1 %copy-start.18 = (s32[1,128,6]{1,0,2:T(1,128)S(1)}, s32[1,128,6]{1,0,2:T(1,128)}, u32[]{:S(2)}) copy-start(s32[1,128,6]{1,0,2:T(1,128)} %param.25) | copy-start | bytes 9220
  446.7 11.3 %copy-start.23 = (f32[1,128,6]{1,0,2:T(1,128)S(1)}, f32[1,128,6]{1,0,2:T(1,128)}, u32[]{:S(2)}) copy-start(f32[1,128,6]{1,0,2:T(1,128)} %param.26) | copy-start | bytes 9220
  446.7 44.3 %all-to-all-start.1 = ((bf16[64,16,640]{2,1,0:T(8,128)(2,1)}), bf16[64,16,640]{2,1,0:T(8,128)(2,1)S(1)}, u32[]{:S(2)}, u32[]{:S(2)}) async-start(bf16[64,16,640]{2,1,0:T(8,128)(2,1)} %bitcast.201), calls=%async_computation.1 | async-start | bytes 2621440 | tf_op jit(solution)/shard_map/all_to_all | solution.py:200
Sparse Core Ops, SparseCore 0:
  9.2 22.2 all-gather.6
  52.1 18.4 all-gather.8
  182.5 69.9 all-reduce.1
  402.7 38.4 all-gather.10
where the time goes:
time: 507 us; the launch traced here: 506 us
  blocking collectives  232 us (46%)
  waiting for transfers between devices  139 us (27%)
  starting transfers between devices  40.3 us (8%)
  matrix products  34.8 us (7%)
  other arithmetic  25.5 us (5%)
  local copies, waits for them, and re-layouts  21 us (4%)
  between operations  13.8 us (3%)
    all_to_all x1, blocking collectives, on_device(): lax.all_to_all(outgoing, ('grp', 'tok'), split_axis=0, concat_axis=0, til...  131 us
    psum x1, waiting for transfers between devices, on_device(): lax.psum(partial_value.astype(jnp.bfloat16), 'head').astype(jnp.float32)  66.5 us
    all_gather x1, blocking collectives, on_device(): lax.all_gather(cached_prefix_values[0], 'tok', axis=0, tiled=True)  39.7 us
    all_gather x1, blocking collectives, on_device(): lax.all_gather(prefix_keys[0], 'tok', axis=0, tiled=True)  39.5 us
    all_gather x1, waiting for transfers between devices, on_device(): lax.all_gather(hidden, 'head', axis=1, tiled=True)  38.6 us
    all_to_all x1, waiting for transfers between devices, on_device(): lax.all_to_all(expert_out, ('grp', 'tok'), split_axis=0, concat_axis=0, t...  32.9 us
    ppermute x8, starting transfers between devices, shifted(): return lax.ppermute(block, axis, route)  29.3 us
    all_gather x1, blocking collectives, on_device(): features = lax.all_gather(quarter, 'head', axis=1, tiled=True)  13.2 us
  transfers between devices with their start and end apart: 13, of which 3 were waited for; matrix products, arithmetic and copies ran while one was open for 9% of the time, Pallas kernels for 0%

commit v1 on v0

--- a/solution.py
+++ b/solution.py
@@ -167,7 +167,9 @@
         attended, full_out, (((1,), (1,)), ((), ())), preferred_element_type=jnp.float32
     )
     share_width = model_width // lax.axis_size("head")
-    mixed_sum = lax.psum(partial_value.astype(jnp.bfloat16), "head").astype(jnp.float32)
+    mixed_sum = jnp.sum(lax.all_gather(partial_value.astype(jnp.bfloat16), "head"), axis=0).astype(
+        jnp.float32
+    )
     mid_full = (features.astype(jnp.float32) + mixed_sum).astype(jnp.bfloat16)
     mid_quarter = lax.dynamic_slice_in_dim(mid_full, head_rank * share_width, share_width, 1)
     moe_in = rms_norm(mid_full, moe_gain)

time: 507 us -> 487 us (0.961)
  waiting for transfers between devices: 139 us -> 126 us
  other arithmetic: 25.5 us -> 20.3 us
    psum x1 -> x0, waiting for transfers between devices: 66.5 us -> none  [on_device(): lax.psum(partial_value.astype(jnp.bfloat16), 'head').astype(jnp.float32)]
    all_gather x0 -> x1, waiting for transfers between devices: none -> 54.3 us  [on_device(): lax.all_gather(partial_value.astype(jnp.bfloat16), 'head')]
  transfers between devices with their start and end apart: 13 -> 13, of which waited for: 3 -> 3; matrix products, arithmetic and copies ran while one was open for 9% -> 8% of each run, Pallas kernels for 0% -> 0%
where the time goes in v1:
time: 487 us; the launch traced here: 485 us
  blocking collectives  230 us (47%)
  waiting for transfers between devices  126 us (26%)
  starting transfers between devices  40.5 us (8%)
  matrix products  34.7 us (7%)
  local copies, waits for them, and re-layouts  20.4 us (4%)
  other arithmetic  20.3 us (4%)
  between operations  13.8 us (3%)
    all_to_all x1, blocking collectives, on_device(): lax.all_to_all(outgoing, ('grp', 'tok'), split_axis=0, concat_axis=0, til...  129 us
    all_gather x1, waiting for transfers between devices, on_device(): lax.all_gather(partial_value.astype(jnp.bfloat16), 'head')  54.3 us
    all_gather x1, blocking collectives, on_device(): lax.all_gather(cached_prefix_values[0], 'tok', axis=0, tiled=True)  39.8 us
    all_gather x1, blocking collectives, on_device(): lax.all_gather(prefix_keys[0], 'tok', axis=0, tiled=True)  39.5 us
    all_gather x1, waiting for transfers between devices, on_device(): lax.all_gather(hidden, 'head', axis=1, tiled=True)  37.9 us
    all_to_all x1, waiting for transfers between devices, on_device(): lax.all_to_all(expert_out, ('grp', 'tok'), split_axis=0, concat_axis=0, t...  32.9 us
    ppermute x8, starting transfers between devices, shifted(): return lax.ppermute(block, axis, route)  29.5 us
    all_gather x1, blocking collectives, on_device(): features = lax.all_gather(quarter, 'head', axis=1, tiled=True)  13.2 us
  transfers between devices with their start and end apart: 13, of which 3 were waited for; matrix products, arithmetic and copies ran while one was open for 8% of the time, Pallas kernels for 0%

profile of v1, /device:TPU:1, one launch (start us, length us, event | category | flops | bytes accessed | tf_op | source)
XLA Modules:
  0.0 485.4 jit_solution(1072868642635604587)
XLA Ops:
  9.6 13.2 %all-gather = bf16[1,128,2560]{2,1,0:T(8,128)(2,1)S(1)} all-gather(bf16[1,128,640]{2,1,0:T(8,128)(2,1)} %param.15), channel_id=2, replica_groups=mesh['grp'=2,'tok'=32,'head'=4] {'head'}, dimensions={2}, use_global_device_ids=true | all-gather | bytes 819200 | tf_op jit(solution)/shard_map/all_gather | solution.py:96
  23.1 6.3 %all_gather.34 = bf16[2560,128]{1,0:T(8,128)(2,1)S(1)} all-gather(bf16[1280,128]{1,0:T(8,128)(2,1)S(1)} %copy-done.2), channel_id=1, replica_groups=mesh['grp'=2,'tok'=32,'head'=4] {'grp'}, dimensions={0}, use_global_device_ids=true | all-gather | bytes 983040 | tf_op jit(solution)/shard_map/all_gather | solution.py:108
  29.3 2.4 all_gather.35
  33.6 1.9 collective-permute-start
  35.5 4.5 collective-permute-start.1
  40.0 4.3 collective-permute-start.2
  44.4 3.6 collective-permute-start.3
  47.9 4.0 collective-permute-start.4
  53.0 39.5 %all-gather.1 = bf16[1,2048,1,128]{3,1,2,0:T(8,128)(2,1)S(1)} all-gather(bf16[1,64,1,128]{3,1,2,0:T(8,128)(2,1)S(1)} %copy-done.15), channel_id=3, replica_groups=mesh['grp'=2,'tok'=32,'head'=4] {'tok'}, dimensions={1}, use_global_device_ids=true | all-gather | bytes 540672 | tf_op jit(solution)/shard_map/all_gather | solution.py:131
  92.5 39.8 %all-gather.2 = bf16[1,2048,1,128]{3,1,2,0:T(8,128)(2,1)} all-gather(bf16[1,64,1,128]{3,1,2,0:T(8,128)(2,1)S(1)} %copy-done.16), channel_id=4, replica_groups=mesh['grp'=2,'tok'=32,'head'=4] {'tok'}, dimensions={1}, use_global_device_ids=true | all-gather | bytes 540672 | tf_op jit(solution)/shard_map/all_gather | solution.py:132
  133.1 3.3 fusion.156
  137.2 1.1 copy.185
  138.3 1.8 copy.186
  140.1 1.1 subtract_convert_fusion
  142.3 3.0 collective-permute-start.5
  145.3 1.0 fusion.169
  146.3 4.9 %collective-permute-start.6 = (bf16[2,128,1,128]{1,3,2,0:T(8,128)(2,1)}, bf16[2,128,1,128]{1,3,2,0:T(8,128)(2,1)S(1)}, u32[]{:S(2)}, u32[]{:S(2)}) collective-permute-start(bf16[2,128,1,128]{1,3,2,0:T(8,128)(2,1)} %pad_maximum_fusion.1), channel_id=1, source_target_pairs={{0,28},{4,32},{8,36},{12,40},{16,44},{20,48},{24,52},{28,56},{32,6... | collective-permute-start | bytes 196616 | tf_op jit(solution)/shard_map/ppermute | solution.py:15
  151.3 1.0 fusion.168
  152.3 3.3 collective-permute-start.7
  155.6 1.0 fusion.167
  156.7 1.0 fusion.166
  157.7 1.0 fusion.165
  160.5 1.0 fusion
  162.5 1.0 fusion.90
  163.5 1.0 fusion.88
  164.5 1.0 fusion.86
  166.2 1.2 fusion.52
  167.6 1.1 fusion.55
  168.8 4.0 convolution_convert_fusion
  173.3 1.8 reduce-window.9
  175.9 3.4 scatter_custom_fusion
  179.4 54.3 %all-gather.15.cloned.1.call-done = bf16[512,2560]{1,0:T(8,128)(2,1)} async-done(((bf16[128,2560]{1,0:T(8,128)(2,1)}), bf16[512,2560]{1,0:T(8,128)(2,1)}) %all-gather.15.cloned.1.call-update) | async-done | bytes 2621456 | tf_op jit(solution)/shard_map/all_gather | solution.py:170
  233.7 2.2 reduce_sum.149
  235.9 1.1 fusion.17
  237.0 1.3 fusion.19
  238.3 6.3 %gather_fusion = bf16[1024,2560]{1,0:T(8,128)(2,1)} fusion(bf16[128,2560]{1,0:T(8,128)(2,1)S(1)} %fusion.19, s32[1024]{0:T(1024)S(1)} %fusion.138), kind=kCustom, calls=%fused_computation | custom fusion | bytes 10489856 | tf_op jit(solution)/shard_map/jit(_take)/gather | solution.py:185
  244.6 2.9 broadcast_select_fusion
  247.5 128.7 %all_to_all.10 = bf16[64,16,2560]{2,1,0:T(8,128)(2,1)S(1)} all-to-all(bf16[64,16,2560]{2,1,0:T(8,128)(2,1)S(1)} %broadcast_select_fusion), channel_id=1, replica_groups=mesh['grp'=2,'tok'=32,'head'=4] {'grp','tok'}, dimensions={0} | all-to-all | bytes 10485760 | tf_op jit(solution)/shard_map/all_to_all | solution.py:188
  376.2 2.9 fusion.10
  379.1 3.8 multiply_convert_fusion
  382.9 37.9 %all-gather.13.cloned.1.call-done = bf16[1024,1536]{1,0:T(8,128)(2,1)} async-done(((bf16[1024,384]{1,0:T(8,128)(2,1)}), bf16[1024,1536]{1,0:T(8,128)(2,1)}) %all-gather.13.cloned.1.call-update) | async-done | bytes 3145744 | tf_op jit(solution)/shard_map/all_gather | solution.py:195
  420.9 5.6 %fusion.12 = bf16[1024,640]{1,0:T(8,128)(2,1)} fusion(bf16[1024,1536]{1,0:T(8,128)(2,1)} %all-gather.13.cloned.1.call-done, bf16[1,1536,640]{2,1,0:T(8,128)(2,1)S(1)} %copy-done), kind=kOutput, calls=%fused_computation.24 | convolution fusion | flops 2013921280 | bytes 6422528 | tf_op jit(solution)/shard_map/dot_general | solution.py:194
  426.5 10.9 %all-to-all-start.1 = ((bf16[64,16,640]{2,1,0:T(8,128)(2,1)}), bf16[64,16,640]{2,1,0:T(8,128)(2,1)S(1)}, u32[]{:S(2)}, u32[]{:S(2)}) async-start(bf16[64,16,640]{2,1,0:T(8,128)(2,1)} %bitcast.203), calls=%async_computation.1 | async-start | bytes 2621440 | tf_op jit(solution)/shard_map/all_to_all | solution.py:202
  437.9 32.9 %all-to-all-done.1 = bf16[64,16,640]{2,1,0:T(8,128)(2,1)S(1)} async-done(((bf16[64,16,640]{2,1,0:T(8,128)(2,1)}), bf16[64,16,640]{2,1,0:T(8,128)(2,1)S(1)}, u32[]{:S(2)}, u32[]{:S(2)}) %all-to-all-start.1) | async-done | bytes 1310752 | tf_op jit(solution)/shard_map/all_to_all | solution.py:202
  470.8 3.4 gather_fusion.1
  474.2 2.1 gather.15
  476.2 1.0 multiply_reduce_fusion.1
  477.3 1.6 fusion.96
  (126 shorter events, 14.2 us)
Async XLA Ops:
  6.5 414.4 %copy-start = (bf16[1,1536,640]{2,1,0:T(8,128)(2,1)S(1)}, bf16[1,1536,640]{2,1,0:T(8,128)(2,1)}, u32[]{:S(2)}) copy-start(bf16[1,1536,640]{2,1,0:T(8,128)(2,1)} %param.29) | copy-start | bytes 5898244
  6.5 16.5 %copy-start.2 = (bf16[1280,128]{1,0:T(8,128)(2,1)S(1)}, bf16[1280,128]{1,0:T(8,128)(2,1)}, u32[]{:S(2)}) copy-start(bf16[1280,128]{1,0:T(8,128)(2,1)} %param.18) | copy-start | bytes 983044
  6.5 22.8 %copy-start.3 = (bf16[1280,128]{1,0:T(8,128)(2,1)S(1)}, bf16[1280,128]{1,0:T(8,128)(2,1)}, u32[]{:S(2)}) copy-start(bf16[1280,128]{1,0:T(8,128)(2,1)} %param.19) | copy-start | bytes 983044
  6.5 126.6 %all-gather.9.cloned.1.call-start = ((), (), s32[]{:S(2)}) async-start(), calls=%async_computation.2 | async-start | bytes 4915200 | tf_op jit(solution)/shard_map/all_gather | solution.py:107
  7.3 161.5 %all-gather.11.cloned.1.call-start = ((), (), s32[]{:S(2)}) async-start(), calls=%async_computation.3 | async-start | bytes 4915200 | tf_op jit(solution)/shard_map/all_gather | solution.py:110
  32.2 20.9 %copy-start.15 = (bf16[1,64,1,128]{3,1,2,0:T(8,128)(2,1)S(1)}, bf16[1,64,1,128]{3,1,2,0:T(8,128)(2,1)}, u32[]{:S(2)}) copy-start(bf16[1,64,1,128]{3,1,2,0:T(8,128)(2,1)} %param.21) | copy-start | bytes 49156
  32.4 0.6 copy-start.8
  32.4 1.2 copy-start.10
  32.4 60.1 %copy-start.16 = (bf16[1,64,1,128]{3,1,2,0:T(8,128)(2,1)S(1)}, bf16[1,64,1,128]{3,1,2,0:T(8,128)(2,1)}, u32[]{:S(2)}) copy-start(bf16[1,64,1,128]{3,1,2,0:T(8,128)(2,1)} %param.22) | copy-start | bytes 49156
  32.9 2.6 copy-start.12
  33.6 108.7 %collective-permute-start = (bf16[2,128,1,128]{1,3,2,0:T(8,128)(2,1)}, bf16[2,128,1,128]{1,3,2,0:T(8,128)(2,1)}, u32[]{:S(2)}, u32[]{:S(2)}) collective-permute-start(bf16[2,128,1,128]{1,3,2,0:T(8,128)(2,1)} %pad_maximum_fusion.1), channel_id=1, source_target_pairs={{0,4},{4,8},{8,12},{12,16},{16,20},{20,24},{24,28},{28,32},{32,36}... | collective-permute-start | bytes 196616 | tf_op jit(solution)/shard_map/ppermute | solution.py:15
  35.5 110.8 %collective-permute-start.1 = (bf16[2,128,1,128]{1,3,2,0:T(8,128)(2,1)}, bf16[2,128,1,128]{1,3,2,0:T(8,128)(2,1)}, u32[]{:S(2)}, u32[]{:S(2)}) collective-permute-start(bf16[2,128,1,128]{1,3,2,0:T(8,128)(2,1)} %pad_maximum_fusion.1), channel_id=1, source_target_pairs={{0,8},{4,12},{8,16},{12,20},{16,24},{20,28},{24,32},{28,36},{32,40... | collective-permute-start | bytes 196616 | tf_op jit(solution)/shard_map/ppermute | solution.py:15
  40.0 112.3 %collective-permute-start.2 = (bf16[2,128,1,128]{1,3,2,0:T(8,128)(2,1)}, bf16[2,128,1,128]{1,3,2,0:T(8,128)(2,1)}, u32[]{:S(2)}, u32[]{:S(2)}) collective-permute-start(bf16[2,128,1,128]{1,3,2,0:T(8,128)(2,1)} %pad_maximum_fusion.1), channel_id=1, source_target_pairs={{0,12},{4,16},{8,20},{12,24},{16,28},{20,32},{24,36},{28,40},{32,4... | collective-permute-start | bytes 196616 | tf_op jit(solution)/shard_map/ppermute | solution.py:15
  44.4 112.3 %collective-permute-start.3 = (bf16[2,128,1,128]{1,3,2,0:T(8,128)(2,1)}, bf16[2,128,1,128]{1,3,2,0:T(8,128)(2,1)}, u32[]{:S(2)}, u32[]{:S(2)}) collective-permute-start(bf16[2,128,1,128]{1,3,2,0:T(8,128)(2,1)} %pad_maximum_fusion.1), channel_id=1, source_target_pairs={{0,16},{4,20},{8,24},{12,28},{16,32},{20,36},{24,40},{28,44},{32,4... | collective-permute-start | bytes 196616 | tf_op jit(solution)/shard_map/ppermute | solution.py:15
  47.9 109.7 %collective-permute-start.4 = (bf16[2,128,1,128]{1,3,2,0:T(8,128)(2,1)}, bf16[2,128,1,128]{1,3,2,0:T(8,128)(2,1)}, u32[]{:S(2)}, u32[]{:S(2)}) collective-permute-start(bf16[2,128,1,128]{1,3,2,0:T(8,128)(2,1)} %pad_maximum_fusion.1), channel_id=1, source_target_pairs={{0,20},{4,24},{8,28},{12,32},{16,36},{20,40},{24,44},{28,48},{32,5... | collective-permute-start | bytes 196616 | tf_op jit(solution)/shard_map/ppermute | solution.py:15
  51.9 181.7 %all-gather.15.cloned.1.call-start = ((), (), s32[]{:S(2)}) async-start(), calls=%async_computation.5 | async-start | bytes 3276800 | tf_op jit(solution)/shard_map/all_gather | solution.py:170
  141.3 10.0 %copy-start.7 = (pred[128,128]{0,1:T(8,128)(4,1)S(1)}, pred[128,128]{0,1:T(8,128)(4,1)}, u32[]{:S(2)}) copy-start(pred[128,128]{0,1:T(8,128)(4,1)} %get-tuple-element.42) | copy-start | bytes 49156
  141.3 14.3 %copy-start.6 = (pred[128,128]{0,1:T(8,128)(4,1)S(1)}, pred[128,128]{0,1:T(8,128)(4,1)}, u32[]{:S(2)}) copy-start(pred[128,128]{0,1:T(8,128)(4,1)} %get-tuple-element.35) | copy-start | bytes 49156
  141.3 15.3 %copy-start.5 = (pred[128,128]{0,1:T(8,128)(4,1)S(1)}, pred[128,128]{0,1:T(8,128)(4,1)}, u32[]{:S(2)}) copy-start(pred[128,128]{0,1:T(8,128)(4,1)} %get-tuple-element.36) | copy-start | bytes 49156
  142.3 15.4 %copy-start.4 = (pred[128,128]{0,1:T(8,128)(4,1)S(1)}, pred[128,128]{0,1:T(8,128)(4,1)}, u32[]{:S(2)}) copy-start(pred[128,128]{0,1:T(8,128)(4,1)} %get-tuple-element.37) | copy-start | bytes 49156
  142.3 17.0 %copy-start.9 = (bf16[128,1,64]{0,2,1:T(8,128)(2,1)S(1)}, bf16[128,1,64]{0,2,1:T(8,128)(2,1)}, u32[]{:S(2)}) copy-start(bf16[128,1,64]{0,2,1:T(8,128)(2,1)} %copy-done.8) | copy-start | bytes 49156
  142.3 17.0 %copy-start.11 = (bf16[128,1,64]{0,2,1:T(8,128)(2,1)S(1)}, bf16[128,1,64]{0,2,1:T(8,128)(2,1)}, u32[]{:S(2)}) copy-start(bf16[128,1,64]{0,2,1:T(8,128)(2,1)} %copy-done.10) | copy-start | bytes 49156
  142.3 16.4 %collective-permute-start.5 = (bf16[2,128,1,128]{1,3,2,0:T(8,128)(2,1)}, bf16[2,128,1,128]{1,3,2,0:T(8,128)(2,1)S(1)}, u32[]{:S(2)}, u32[]{:S(2)}) collective-permute-start(bf16[2,128,1,128]{1,3,2,0:T(8,128)(2,1)} %pad_maximum_fusion.1), channel_id=1, source_target_pairs={{0,24},{4,28},{8,32},{12,36},{16,40},{20,44},{24,48},{28,52},{32,5... | collective-permute-start | bytes 196616 | tf_op jit(solution)/shard_map/ppermute | solution.py:15
  146.3 12.6 %collective-permute-start.6 = (bf16[2,128,1,128]{1,3,2,0:T(8,128)(2,1)}, bf16[2,128,1,128]{1,3,2,0:T(8,128)(2,1)S(1)}, u32[]{:S(2)}, u32[]{:S(2)}) collective-permute-start(bf16[2,128,1,128]{1,3,2,0:T(8,128)(2,1)} %pad_maximum_fusion.1), channel_id=1, source_target_pairs={{0,28},{4,32},{8,36},{12,40},{16,44},{20,48},{24,52},{28,56},{32,6... | collective-permute-start | bytes 196616 | tf_op jit(solution)/shard_map/ppermute | solution.py:15
  152.3 7.2 %collective-permute-start.7 = (bf16[2,128,1,128]{1,3,2,0:T(8,128)(2,1)}, bf16[2,128,1,128]{1,3,2,0:T(8,128)(2,1)S(1)}, u32[]{:S(2)}, u32[]{:S(2)}) collective-permute-start(bf16[2,128,1,128]{1,3,2,0:T(8,128)(2,1)} %pad_maximum_fusion.1), channel_id=1, source_target_pairs={{0,32},{4,36},{8,40},{12,44},{16,48},{20,52},{24,56},{28,60},{32,6... | collective-permute-start | bytes 196616 | tf_op jit(solution)/shard_map/ppermute | solution.py:15
  162.5 3.7 copy-start.1
  166.2 1.2 copy-start.13
  168.8 4.1 copy-start.14
  168.8 4.5 copy-start.17
  172.8 248.1 %all-gather.13.cloned.1.call-start = ((), (), s32[]{:S(2)}) async-start(), calls=%async_computation.4 | async-start | bytes 3932160 | tf_op jit(solution)/shard_map/all_gather | solution.py:195
  247.5 128.7 %copy-start.19 = (bf16[1,2560,384]{2,1,0:T(8,128)(2,1)S(1)}, bf16[1,2560,384]{2,1,0:T(8,128)(2,1)}, u32[]{:S(2)}) copy-start(bf16[1,2560,384]{2,1,0:T(8,128)(2,1)} %param.27) | copy-start | bytes 5898244
  376.2 2.9 copy-start.20
  426.5 11.3 %copy-start.18 = (f32[1,128,6]{1,0,2:T(1,128)S(1)}, f32[1,128,6]{1,0,2:T(1,128)}, u32[]{:S(2)}) copy-start(f32[1,128,6]{1,0,2:T(1,128)} %param.26) | copy-start | bytes 9220
  426.5 44.3 %all-to-all-start.1 = ((bf16[64,16,640]{2,1,0:T(8,128)(2,1)}), bf16[64,16,640]{2,1,0:T(8,128)(2,1)S(1)}, u32[]{:S(2)}, u32[]{:S(2)}) async-start(bf16[64,16,640]{2,1,0:T(8,128)(2,1)} %bitcast.203), calls=%async_computation.1 | async-start | bytes 2621440 | tf_op jit(solution)/shard_map/all_to_all | solution.py:202
Sparse Core Ops, SparseCore 0:
  9.2 22.2 all-gather.8
  52.0 18.4 all-gather.10
  172.9 60.6 all-gather.14
  383.1 37.7 all-gather.12
